TPU v7x, 32 devices: a whole 2x2x4 slice. The times are simulated.
32 devices in a mesh: dp: 4 (over z), freq: 2 (over core), tm: 4 (over y, x).
Axes of the slice: x: 2, y: 2, z: 4, core: 2. Of those that a mesh axis runs over, the one named last changes fastest.
Arguments:
- patches: bfloat16 [1312, 32, 768], P(('freq', 'tm'), 'dp'), may hold values from -6 to 6
- col_counts: int32 [4], replicated, may hold values from 26 to 27, as said below
- norm_gain: bfloat16 [2, 768], replicated, may hold values from 0.099609375 to 1.8984375
- norm_shift: bfloat16 [2, 768], replicated, may hold values from -3 to 3
- joint_proj: bfloat16 [768, 2304], replicated, may hold values from -0.3125 to 0.3125
- proj_bias: bfloat16 [2, 768], replicated, may hold values from -3 to 3
- out_proj: bfloat16 [768, 768], replicated, may hold values from -0.875 to 0.875
- up_proj: bfloat16 [768, 3072], replicated, may hold values from -0.21875 to 0.21875
- up_bias: bfloat16 [3072], replicated, may hold values from -3 to 3
- down_proj: bfloat16 [3072, 768], replicated, may hold values from -0.109375 to 0.109375
- out_bias: bfloat16 [2, 768], replicated, may hold values from -3 to 3
- cotangent: bfloat16 [1312, 32, 768], P(('freq', 'tm'), 'dp'), may hold values from -6 to 6
Outputs:
- output: bfloat16 [1312, 32, 768], P(('freq', 'tm'), 'dp')
- grad_patches: bfloat16 [1312, 32, 768], P(('freq', 'tm'), 'dp')
- grad_norm_gain: float32 [2, 768], P(None, ('freq', 'tm'))
- grad_norm_shift: float32 [2, 768], P(None, ('freq', 'tm'))
- grad_joint_proj: float32 [768, 2304], P(('freq', 'tm'))
- grad_proj_bias: float32 [2, 768], P(None, ('freq', 'tm'))
- grad_out_proj: float32 [768, 768], P(('freq', 'tm'))
- grad_up_proj: float32 [768, 3072], P(('freq', 'tm'))
- grad_up_bias: float32 [3072], P(('freq', 'tm'))
- grad_down_proj: float32 [3072, 768], P(('freq', 'tm'))
- grad_out_bias: float32 [2, 768], P(None, ('freq', 'tm'))
Inputs may be any that keep to these rules, and one draw needn't show every extreme that they name: `col_counts`: each entry is 26 or 27, and both occur in every draw.
All inputs are finite; a program needn't handle non-finite values.
Results may differ from a plain program's by a relative error of at most 0.019.
Values may be sent and summed in bfloat16 or wider, within the bound.
No kernel may reach another device: no remote copies, remote signals or barrier semaphores. Data moves between devices by JAX's collectives and lax.ppermute only.
A program may use at most 448 MiB of HBM per device.

v0:
```python
import math
import jax
import jax.numpy as jnp
from jax import lax
from jax.sharding import PartitionSpec as P

HEADS = 12
DH = 64
FREQ_ROWS = 12
EPS = 1e-06
NEG = -1000000000.0


def live_slots(col_counts, slot_ids, freq_ids, time_ids, freq_rows, cap_cols):
    table = jnp.arange(col_counts.shape[0], dtype=jnp.int32)
    live_cols = jnp.sum(
        jnp.where(time_ids[:, None] == table[None, :], col_counts[None, :], 0), axis=1
    )
    in_grid = slot_ids < freq_rows * cap_cols
    column_live = slot_ids // freq_rows < live_cols
    extra_live = (time_ids == 0) & (freq_ids == 0)
    return jnp.where(in_grid, column_live, extra_live)


def norm_rows(values, gain, shift):
    centered = values - jnp.mean(values, axis=-1, keepdims=True)
    inverse = lax.rsqrt(jnp.mean(centered * centered, axis=-1, keepdims=True) + EPS)
    return centered * inverse * gain + shift


def gelu_exact(values):
    return jax.nn.gelu(values, approximate=False)


def matmul(left, right):
    return jnp.dot(left, right, preferred_element_type=jnp.float32)


def matmul_tn(left, right):
    return lax.dot_general(
        left, right, (((0,), (0,)), ((), ())), preferred_element_type=jnp.float32
    )


def matmul_nt(left, right):
    return lax.dot_general(
        left, right, (((1,), (1,)), ((), ())), preferred_element_type=jnp.float32
    )


def head_pair(array, offset, lane_width, head_size):
    section = lax.dynamic_slice_in_dim(array, offset, lane_width, 2)
    return section.reshape(section.shape[0], section.shape[1], 2, head_size)


def add_lanes(target, addend, offset):
    current = lax.dynamic_slice_in_dim(target, offset, addend.shape[2], 2)
    return lax.dynamic_update_slice_in_dim(target, current + addend, offset, 2)


def pair_probs(query_pair, key_pair, log_pair, mask, scale):
    scores = (
        jnp.einsum("qchd,kchd->chqk", query_pair, key_pair, preferred_element_type=jnp.float32)
        * scale
        + mask
    )
    return jnp.exp(scores - jnp.transpose(log_pair, (1, 2, 0))[..., None])


def per_device(
    patches,
    col_counts,
    norm_gain,
    norm_shift,
    joint_proj,
    proj_bias,
    out_proj,
    up_proj,
    up_bias,
    down_proj,
    out_bias,
    cotangent,
):
    slots, clips, width = patches.shape
    row_count = slots * clips
    lane_width = 2 * DH
    pair_count = HEADS // 2
    scale = 1.0 / math.sqrt(DH)
    freq_size = lax.axis_size("freq")
    time_size = lax.axis_size("tm")
    freq_rows = FREQ_ROWS // freq_size
    cap_cols = (slots - 2) // freq_rows
    key_count = slots * freq_size * time_size
    slot_ids = jnp.arange(slots, dtype=jnp.int32)
    own_live = live_slots(
        col_counts,
        slot_ids,
        jnp.full((slots,), lax.axis_index("freq"), jnp.int32),
        jnp.full((slots,), lax.axis_index("tm"), jnp.int32),
        freq_rows,
        cap_cols,
    )
    key_ids = jnp.arange(key_count, dtype=jnp.int32)
    key_group = key_ids // slots
    key_live = live_slots(
        col_counts,
        key_ids % slots,
        key_group // time_size,
        key_group % time_size,
        freq_rows,
        cap_cols,
    )
    key_mask = jnp.where(key_live, 0.0, NEG).astype(jnp.float32)
    row_live = (
        jnp.broadcast_to(own_live[:, None], (slots, clips))
        .reshape(row_count, 1)
        .astype(jnp.float32)
    )
    gain_full = norm_gain.astype(jnp.float32)
    shift_full = norm_shift.astype(jnp.float32)
    bias_full = proj_bias.astype(jnp.float32)
    outb_full = out_bias.astype(jnp.float32)
    upb_full = up_bias.astype(jnp.float32)
    inputs = patches.reshape(row_count, width).astype(jnp.float32)
    normed1, ln1_back = jax.vjp(norm_rows, inputs, gain_full[0], shift_full[0])
    normed1_low = normed1.astype(jnp.bfloat16)
    joint = matmul(normed1_low, joint_proj)
    query_low = (joint[:, :width] + bias_full[0]).astype(jnp.bfloat16)
    keys_low = joint[:, width : 2 * width].astype(jnp.bfloat16)
    memory_low = (joint[:, 2 * width :] + bias_full[1]).astype(jnp.bfloat16)
    query3 = query_low.reshape(slots, clips, width)
    key_value = jnp.concatenate([keys_low, memory_low], axis=1).reshape(slots, clips, 2 * width)
    all_memory = lax.all_gather(key_value, ("freq", "tm"), axis=0, tiled=True)

    def forward_pair(number, state):
        mixed_acc, log_acc = state
        offset = number * lane_width
        query_pair = head_pair(query3, offset, lane_width, DH)
        key_pair = head_pair(all_memory, offset, lane_width, DH)
        value_pair = head_pair(all_memory, width + offset, lane_width, DH)
        scores = (
            jnp.einsum("qchd,kchd->chqk", query_pair, key_pair, preferred_element_type=jnp.float32)
            * scale
            + key_mask
        )
        highest = jnp.max(scores, axis=-1, keepdims=True)
        exponent = jnp.exp(scores - highest)
        summed = jnp.sum(exponent, axis=-1, keepdims=True)
        attention = (exponent / summed).astype(jnp.bfloat16)
        mixed = jnp.einsum(
            "chqk,kchd->qchd", attention, value_pair, preferred_element_type=jnp.float32
        )
        log_pair = jnp.transpose((highest + jnp.log(summed))[..., 0], (2, 0, 1))
        mixed_acc = lax.dynamic_update_slice_in_dim(
            mixed_acc, mixed.reshape(slots, clips, lane_width), offset, 2
        )
        log_acc = lax.dynamic_update_slice_in_dim(log_acc, log_pair, 2 * number, 2)
        return (mixed_acc, log_acc)

    mixed_full, log_rows = lax.fori_loop(
        0,
        pair_count,
        forward_pair,
        (
            jnp.zeros((slots, clips, width), jnp.float32),
            jnp.zeros((slots, clips, HEADS), jnp.float32),
        ),
    )
    mixed_low = mixed_full.reshape(row_count, width).astype(jnp.bfloat16)
    middle = inputs + matmul(mixed_low, out_proj) + outb_full[0]
    normed2, ln2_back = jax.vjp(norm_rows, middle, gain_full[1], shift_full[1])
    normed2_low = normed2.astype(jnp.bfloat16)
    pre_act = matmul(normed2_low, up_proj) + upb_full
    activated, gelu_back = jax.vjp(gelu_exact, pre_act)
    hidden_low = activated.astype(jnp.bfloat16)
    final = middle + matmul(hidden_low, down_proj) + outb_full[1]
    output = (final * row_live).astype(jnp.bfloat16).reshape(slots, clips, width)
    grad_out_rows = cotangent.reshape(row_count, width).astype(jnp.float32) * row_live
    grad_out_low = grad_out_rows.astype(jnp.bfloat16)
    grad_down_part = matmul_tn(hidden_low, grad_out_low)
    grad_outb_mlp = jnp.sum(grad_out_rows, axis=0)
    grad_hidden = matmul_nt(grad_out_low, down_proj)
    grad_pre_low = gelu_back(grad_hidden)[0].astype(jnp.bfloat16)
    grad_up_part = matmul_tn(normed2_low, grad_pre_low)
    grad_upb_part = jnp.sum(grad_pre_low.astype(jnp.float32), axis=0)
    grad_normed2 = matmul_nt(grad_pre_low, up_proj)
    grad_mid_part, grad_gain_mlp, grad_shift_mlp = ln2_back(grad_normed2)
    grad_middle = grad_out_rows + grad_mid_part
    grad_branch = grad_middle.astype(jnp.bfloat16)
    grad_outp_part = matmul_tn(mixed_low, grad_branch)
    grad_outb_attn = jnp.sum(grad_branch.astype(jnp.float32), axis=0)
    grad_mixed_low = matmul_nt(grad_branch, out_proj).astype(jnp.bfloat16)
    grad_mixed3 = grad_mixed_low.reshape(slots, clips, width)

    def query_side(number):
        offset = number * lane_width
        query_pair = head_pair(query3, offset, lane_width, DH)
        grad_pair = head_pair(grad_mixed3, offset, lane_width, DH)
        key_pair = head_pair(all_memory, offset, lane_width, DH)
        value_pair = head_pair(all_memory, width + offset, lane_width, DH)
        log_pair = lax.dynamic_slice_in_dim(log_rows, 2 * number, 2, 2)
        probability = pair_probs(query_pair, key_pair, log_pair, key_mask, scale)
        grad_probs = jnp.einsum(
            "qchd,kchd->chqk", grad_pair, value_pair, preferred_element_type=jnp.float32
        )
        delta = jnp.sum(probability * grad_probs, axis=-1, keepdims=True)
        grad_scores = (probability * (grad_probs - delta)).astype(jnp.bfloat16)
        grad_query = (
            jnp.einsum("chqk,kchd->qchd", grad_scores, key_pair, preferred_element_type=jnp.float32)
            * scale
        )
        return (
            offset,
            query_pair,
            grad_pair,
            probability,
            grad_scores,
            delta,
            grad_query.reshape(slots, clips, lane_width),
        )

    zero_query = jnp.zeros((slots, clips, width), jnp.float32)

    def backward_pair(number, state):
        grad_query_acc, grad_memory = state
        side = query_side(number)
        offset = side[0]
        grad_keys = (
            jnp.einsum("chqk,qchd->kchd", side[4], side[1], preferred_element_type=jnp.float32)
            * scale
        )
        grad_values = jnp.einsum(
            "chqk,qchd->kchd",
            side[3].astype(jnp.bfloat16),
            side[2],
            preferred_element_type=jnp.float32,
        )
        grad_memory = add_lanes(
            grad_memory, grad_keys.reshape(key_count, clips, lane_width), offset
        )
        grad_memory = add_lanes(
            grad_memory, grad_values.reshape(key_count, clips, lane_width), width + offset
        )
        return (add_lanes(grad_query_acc, side[6], offset), grad_memory)

    grad_query_full, grad_memory_all = lax.fori_loop(
        0,
        pair_count,
        backward_pair,
        (zero_query, jnp.zeros((key_count, clips, 2 * width), jnp.float32)),
    )
    grad_memory_own = lax.psum_scatter(
        grad_memory_all, ("freq", "tm"), scatter_dimension=0, tiled=True
    )
    grad_query_low = grad_query_full.reshape(row_count, width).astype(jnp.bfloat16)
    grad_memory_low = grad_memory_own.reshape(row_count, 2 * width).astype(jnp.bfloat16)
    grad_joint = jnp.concatenate([grad_query_low, grad_memory_low], axis=1)
    grad_joint_part = matmul_tn(normed1_low, grad_joint)
    grad_bias_cols = jnp.stack(
        [
            jnp.sum(grad_query_low.astype(jnp.float32), axis=0),
            jnp.sum(grad_memory_low[:, width:].astype(jnp.float32), axis=0),
        ],
        axis=1,
    )
    grad_normed1 = matmul_nt(grad_joint, joint_proj)
    grad_in_part, grad_gain_attn, grad_shift_attn = ln1_back(grad_normed1)
    grad_patches = (grad_middle + grad_in_part).astype(jnp.bfloat16).reshape(slots, clips, width)
    shares = (
        lax.psum_scatter(
            grad_joint_part.astype(jnp.bfloat16), ("freq", "tm"), scatter_dimension=0, tiled=True
        ).astype(jnp.float32),
        lax.psum_scatter(
            grad_bias_cols.astype(jnp.bfloat16), ("freq", "tm"), scatter_dimension=0, tiled=True
        ).astype(jnp.float32),
        lax.psum_scatter(
            grad_outp_part.astype(jnp.bfloat16), ("freq", "tm"), scatter_dimension=0, tiled=True
        ).astype(jnp.float32),
        lax.psum_scatter(
            grad_outb_attn.astype(jnp.bfloat16), ("freq", "tm"), scatter_dimension=0, tiled=True
        ).astype(jnp.float32),
        lax.psum_scatter(
            grad_gain_attn.astype(jnp.bfloat16), ("freq", "tm"), scatter_dimension=0, tiled=True
        ).astype(jnp.float32),
        lax.psum_scatter(
            grad_shift_attn.astype(jnp.bfloat16), ("freq", "tm"), scatter_dimension=0, tiled=True
        ).astype(jnp.float32),
        lax.psum_scatter(
            grad_up_part.astype(jnp.bfloat16), ("freq", "tm"), scatter_dimension=0, tiled=True
        ).astype(jnp.float32),
        lax.psum_scatter(
            grad_upb_part.astype(jnp.bfloat16), ("freq", "tm"), scatter_dimension=0, tiled=True
        ).astype(jnp.float32),
        lax.psum_scatter(
            grad_down_part.astype(jnp.bfloat16), ("freq", "tm"), scatter_dimension=0, tiled=True
        ).astype(jnp.float32),
        lax.psum_scatter(
            grad_outb_mlp.astype(jnp.bfloat16), ("freq", "tm"), scatter_dimension=0, tiled=True
        ).astype(jnp.float32),
        lax.psum_scatter(
            grad_gain_mlp.astype(jnp.bfloat16), ("freq", "tm"), scatter_dimension=0, tiled=True
        ).astype(jnp.float32),
        lax.psum_scatter(
            grad_shift_mlp.astype(jnp.bfloat16), ("freq", "tm"), scatter_dimension=0, tiled=True
        ).astype(jnp.float32),
    )
    summed_all = (
        lax.psum(shares[0].astype(jnp.bfloat16), "dp").astype(jnp.float32),
        lax.psum(shares[1].astype(jnp.bfloat16), "dp").astype(jnp.float32),
        lax.psum(shares[2].astype(jnp.bfloat16), "dp").astype(jnp.float32),
        lax.psum(shares[3].astype(jnp.bfloat16), "dp").astype(jnp.float32),
        lax.psum(shares[4].astype(jnp.bfloat16), "dp").astype(jnp.float32),
        lax.psum(shares[5].astype(jnp.bfloat16), "dp").astype(jnp.float32),
        lax.psum(shares[6].astype(jnp.bfloat16), "dp").astype(jnp.float32),
        lax.psum(shares[7].astype(jnp.bfloat16), "dp").astype(jnp.float32),
        lax.psum(shares[8].astype(jnp.bfloat16), "dp").astype(jnp.float32),
        lax.psum(shares[9].astype(jnp.bfloat16), "dp").astype(jnp.float32),
        lax.psum(shares[10].astype(jnp.bfloat16), "dp").astype(jnp.float32),
        lax.psum(shares[11].astype(jnp.bfloat16), "dp").astype(jnp.float32),
    )
    attn_summed = summed_all[:6]
    mlp_summed = summed_all[6:]
    grad_norm_gain = jnp.stack([attn_summed[4], mlp_summed[4]])
    grad_norm_shift = jnp.stack([attn_summed[5], mlp_summed[5]])
    grad_out_bias = jnp.stack([attn_summed[3], mlp_summed[3]])
    grad_proj_bias = jnp.transpose(attn_summed[1])
    return (
        output,
        grad_patches,
        grad_norm_gain,
        grad_norm_shift,
        attn_summed[0],
        grad_proj_bias,
        attn_summed[2],
        mlp_summed[0],
        mlp_summed[1],
        mlp_summed[2],
        grad_out_bias,
    )


def solution(mesh):
    return jax.shard_map(
        per_device,
        mesh=mesh,
        in_specs=(
            P(("freq", "tm"), "dp", None),
            P(),
            P(),
            P(),
            P(),
            P(),
            P(),
            P(),
            P(),
            P(),
            P(),
            P(("freq", "tm"), "dp", None),
        ),
        out_specs=(
            P(("freq", "tm"), "dp", None),
            P(("freq", "tm"), "dp", None),
            P(None, ("freq", "tm")),
            P(None, ("freq", "tm")),
            P(("freq", "tm"), None),
            P(None, ("freq", "tm")),
            P(("freq", "tm"), None),
            P(("freq", "tm"), None),
            P(("freq", "tm")),
            P(("freq", "tm"), None),
            P(None, ("freq", "tm")),
        ),
        check_vma=False,
    )
```

profile of v0, /device:TPU:0, one launch (start us, length us, event | category | flops | bytes accessed | tf_op | source)
XLA Modules:
  0.0 1731.1 jit_solution(16705769092683540999)
XLA Ops:
  44.3 144.5 %all-gather.2.cloned.1.call-done = bf16[1312,8,1536]{2,1,0:T(8,128)(2,1)} async-done(((bf16[164,8,1536]{2,1,0:T(8,128)(2,1)}), bf16[1312,8,1536]{2,1,0:T(8,128)(2,1)}) %all-gather.2.cloned.1.call-update) | async-done | bytes 32243728 | tf_op jit(solution)/shard_map/all_gather | solution.py:133
  188.8 42.4 %copy.42 = bf16[1312,8,1536]{0,2,1:T(8,128)(2,1)} copy(bf16[1312,8,1536]{2,1,0:T(8,128)(2,1)} %all-gather.2.cloned.1.call-done) | data formatting | bytes 64487424 | tf_op jit(solution)/shard_map/while | solution.py:160
  231.9 122.6 %while.34 = (s32[]{:T(128)}, bf16[164,8,768]{2,1,0:T(8,128)(2,1)}, f32[164,8,12]{0,2,1:T(8,128)}, bf16[1312,8,1536]{0,2,1:T(8,128)(2,1)}, bf16[164,8,768]{0,2,1:...) while((s32[]{:T(128)}, bf16[164,8,768]{2,1,0:T(8,128)(2,1)}, ...), condition=%wide.region_6.7_spmd, body=%wide.region_3.6_spmd.sunk | while | flops 922637760 | bytes 60295916 | solution.py:160
  360.4 45.8 %multiply_convert_fusion.1 = (bf16[1312,3072]{1,0:T(8,128)(2,1)}, f32[1312,3072]{1,0:T(8,128)}, f32[1312,3072]{1,0:T(8,128)}) fusion(f32[3072]{0:T(1024)S(1)} %copy-done.41, bf16[768,3072]{1,0:T(8,128)(2,1)S(1)} %bitcast.204, f32[1312,768]{1,0:T(8,128)S(1)} %get-tuple-element.504, f32[768]{0:T(1024)S(1)} %copy-done.46, f32[768]{0:T(1024)S(1)} %copy-done.39, ...), kind=kOutput, calls=%fused_computation.34 | convolution fusion | flops 6461841408 | bytes 49082624 | tf_op jit(solution)/shard_map/dot_general | solution.py:36
  406.3 21.5 %fusion.75 = (bf16[3072]{0:T(1024)(128)(2,1)}, bf16[1312,3072]{1,0:T(8,128)(2,1)}) fusion(f32[1312,3072]{1,0:T(8,128)} %get-tuple-element.492, bf16[3072,768]{1,0:T(8,128)(2,1)} %param.25, bf16[164,8,768]{2,1,0:T(8,128)(2,1)} %param.27, f32[1312]{0:T(1024)S(1)} %copy-done.22, f32[1312,3072]{1,0:T(8,128)} %get-tuple-element.505, f32[3072]{0:T(1024)} %convert_element_type.229), kind=kOutput, calls=%fused_computation.178 | convolution fusion | flops 6258299904 | bytes 47062144 | tf_op jit(solution)/shard_map/dot_general | solution.py:46
  427.8 14.1 multiply_reduce_fusion.1
  451.1 21.7 %broadcast_in_dim.96 = f32[1312,8,1536]{0,2,1:T(8,128)} broadcast(f32[]{:T(128)} %constant.301.clone.1), dimensions={} | broadcast | bytes 64487428 | tf_op jit(solution)/shard_map/broadcast_in_dim | solution.py:250
  472.7 478.7 %while.35 = (s32[]{:T(128)}, f32[164,8,768]{2,1,0:T(8,128)}, f32[1312,8,1536]{0,2,1:T(8,128)}, bf16[1312,8,1536]{0,2,1:T(8,128)(2,1)}, bf16[164,8,768]{0,2,1:T(8...) while((s32[]{:T(128)}, f32[164,8,768]{2,1,0:T(8,128)}, ...), condition=%wide.region_14.15_spmd, body=%wide.region_12.14_spmd.sunk | while | flops 2238668288 | bytes 267073456 | solution.py:246
  495.4 11.0 multiply_reduce_fusion.5
  506.5 10.5 multiply_convert_fusion.4
  575.2 11.0 multiply_reduce_fusion.5
  586.2 10.5 multiply_convert_fusion.4
  655.0 11.0 multiply_reduce_fusion.5
  666.0 10.5 multiply_convert_fusion.4
  734.7 11.0 multiply_reduce_fusion.5
  745.8 10.5 multiply_convert_fusion.4
  814.4 11.0 multiply_reduce_fusion.5
  825.5 10.5 multiply_convert_fusion.4
  894.1 11.0 multiply_reduce_fusion.5
  951.5 67.9 %copy.49 = f32[1312,8,1536]{2,1,0:T(8,128)} copy(f32[1312,8,1536]{0,2,1:T(8,128)} %get-tuple-element.368) | data formatting | bytes 128974848 | tf_op jit(solution)/shard_map/while | solution.py:246
  1024.8 12.6 convolution_convert_fusion.2
  1038.1 15.0 convolution_convert_fusion.1
  1057.5 334.1 %reduce-scatter.9.cloned.1.call-done = f32[164,8,1536]{2,1,0:T(8,128)} async-done(((f32[1312,8,1536]{2,1,0:T(8,128)}), f32[164,8,1536]{2,1,0:T(8,128)}) %reduce-scatter.9.cloned.1.call-update) | async-done | bytes 8060944 | tf_op jit(solution)/shard_map/reduce_scatter | solution.py:252
  1414.3 11.5 fusion.40
  1428.3 11.0 fusion.69
  1445.8 27.6 %all-reduce.7 = (bf16[768]{0:T(1024)(128)(2,1)}, bf16[768]{0:T(1024)(128)(2,1)}, bf16[768]{0:T(1024)(128)(2,1)}, bf16[768]{0:T(1024)(128)(2,1)}, bf16[3072]{0:T(...) all-reduce(bf16[768]{0:T(1024)(128)(2,1)} %get-tuple-element.425, ...), channel_id=4, replica_groups=mesh['dp'=4,'freq'=2,'tm'=4] {'freq','tm'}, use_global_device_ids=true, to_apply=%region_22.23.clone | all-reduce | flops 7680 | bytes 30720
  1474.6 15.7 reduce-scatter.17.cloned.1.call-done
  1490.3 57.2 %reduce-scatter.15.cloned.1.call-done = bf16[96,3072]{1,0:T(8,128)(2,1)} async-done(((bf16[768,3072]{1,0:T(8,128)(2,1)}), bf16[96,3072]{1,0:T(8,128)(2,1)}) %reduce-scatter.15.cloned.1.call-update) | async-done | bytes 589840 | tf_op jit(solution)/shard_map/reduce_scatter | solution.py:288
  1547.5 51.8 %reduce-scatter.11.cloned.1.call-done = bf16[96,2304]{1,0:T(8,128)(2,1)} async-done(((bf16[768,2304]{1,0:T(8,128)(2,1)}), bf16[96,2304]{1,0:T(8,128)(2,1)}) %reduce-scatter.11.cloned.1.call-update) | async-done | bytes 442384 | tf_op jit(solution)/shard_map/reduce_scatter | solution.py:270
  1614.4 22.4 %reduce-scatter.19.cloned.1.call-done = bf16[96,2]{1,0:T(8,128)(2,1)} async-done(((bf16[768,2]{1,0:T(8,128)(2,1)}), bf16[96,2]{1,0:T(8,128)(2,1)}) %reduce-scatter.19.cloned.1.call-update) | async-done | bytes 400
  1637.6 12.7 all-reduce.8
  1655.2 60.9 %all-reduce.12.cloned.1.call-done = (bf16[96,2304]{1,0:T(8,128)(2,1)}, bf16[96,768]{1,0:T(8,128)(2,1)}, bf16[96,3072]{1,0:T(8,128)(2,1)}, bf16[384,768]{1,0:T(8,128)(2,1)}) async-done(((bf16[96,2304]{1,0:T(8,128)(2,1)}, bf16[96,768]{1,0:T(8,128)(2,1)}, bf16[96,3072]{1,0:T(8,128)(2,1)}, bf16[384,768]{1,0:T(8,128)(2,1)}), (bf16[96,2304]{1,0:T(8,128)(2,1)}, bf16[96,768]{1,0:T(8,128)(2,1)}, ...) | async-done | bytes 1769488 | tf_op jit(solution)/shard_map/psum | solution.py:308
  (452 shorter events, 604.9 us)
Async XLA Ops:
  7.2 11.6 copy-start
  7.2 181.6 %all-gather.2.cloned.1.call-start = ((), (), s32[]{:S(2)}) async-start(), calls=%async_computation.6 | async-start | bytes 36274176 | tf_op jit(solution)/shard_map/all_gather | solution.py:133
  10.9 14.7 copy-start.20
  30.7 1360.9 %reduce-scatter.9.cloned.1.call-start = ((), (), s32[]{:S(2)}) async-start(), calls=%async_computation.7 | async-start | bytes 72548352 | tf_op jit(solution)/shard_map/reduce_scatter | solution.py:252
  359.1 47.1 %copy-start.9 = (f32[1312,768]{1,0:T(8,128)}, f32[1312,768]{1,0:T(8,128)S(1)}, u32[]{:S(2)}) copy-start(f32[1312,768]{1,0:T(8,128)S(1)} %get-tuple-element.504) | copy-start | bytes 12091396
  359.2 82.8 %copy-start.31 = (f32[1312]{0:T(1024)}, f32[1312]{0:T(1024)S(1)}, u32[]{:S(2)}) copy-start(f32[1312]{0:T(1024)S(1)} %broadcast_multiply_fusion.1) | copy-start | bytes 15748
  359.8 46.5 %copy-start.35 = (f32[1312]{0:T(1024)}, f32[1312]{0:T(1024)S(1)}, u32[]{:S(2)}) copy-start(f32[1312]{0:T(1024)S(1)} %fusion.60) | copy-start | bytes 15748
  360.4 45.9 %copy-start.22 = (f32[1312]{0:T(1024)S(1)}, f32[1312]{0:T(1024)}, u32[]{:S(2)}) copy-start(f32[1312]{0:T(1024)} %convert_element_type.232) | copy-start | bytes 15748
  427.8 14.1 copy-start.28
  427.8 14.2 copy-start.10
  427.8 14.2 copy-start.36
  427.8 14.2 copy-start.40
  451.1 21.7 %copy-start.15 = (f32[1312]{0:T(1024)S(1)}, f32[1312]{0:T(1024)}, u32[]{:S(2)}) copy-start(f32[1312]{0:T(1024)} %get-tuple-element.731) | copy-start | bytes 15748
  487.7 18.7 %copy-start.2 = (bf16[1312,8,128]{0,2,1:T(8,128)(2,1)}, bf16[1312,8,128]{0,2,1:T(8,128)(2,1)S(1)}, u32[]{:S(2)}) copy-start(bf16[1312,8,128]{0,2,1:T(8,128)(2,1)S(1)} %get-tuple-element.610) | copy-start | bytes 8060932 | tf_op jit(solution)/shard_map/while
  506.5 14.0 copy-start.1
  567.5 18.7 %copy-start.2 = (bf16[1312,8,128]{0,2,1:T(8,128)(2,1)}, bf16[1312,8,128]{0,2,1:T(8,128)(2,1)S(1)}, u32[]{:S(2)}) copy-start(bf16[1312,8,128]{0,2,1:T(8,128)(2,1)S(1)} %get-tuple-element.610) | copy-start | bytes 8060932 | tf_op jit(solution)/shard_map/while
  586.2 14.0 copy-start.1
  647.3 18.7 %copy-start.2 = (bf16[1312,8,128]{0,2,1:T(8,128)(2,1)}, bf16[1312,8,128]{0,2,1:T(8,128)(2,1)S(1)}, u32[]{:S(2)}) copy-start(bf16[1312,8,128]{0,2,1:T(8,128)(2,1)S(1)} %get-tuple-element.610) | copy-start | bytes 8060932 | tf_op jit(solution)/shard_map/while
  666.0 14.0 copy-start.1
  727.0 18.7 %copy-start.2 = (bf16[1312,8,128]{0,2,1:T(8,128)(2,1)}, bf16[1312,8,128]{0,2,1:T(8,128)(2,1)S(1)}, u32[]{:S(2)}) copy-start(bf16[1312,8,128]{0,2,1:T(8,128)(2,1)S(1)} %get-tuple-element.610) | copy-start | bytes 8060932 | tf_op jit(solution)/shard_map/while
  745.8 14.0 copy-start.1
  806.7 18.7 %copy-start.2 = (bf16[1312,8,128]{0,2,1:T(8,128)(2,1)}, bf16[1312,8,128]{0,2,1:T(8,128)(2,1)S(1)}, u32[]{:S(2)}) copy-start(bf16[1312,8,128]{0,2,1:T(8,128)(2,1)S(1)} %get-tuple-element.610) | copy-start | bytes 8060932 | tf_op jit(solution)/shard_map/while
  825.5 14.0 copy-start.1
  886.4 18.7 %copy-start.2 = (bf16[1312,8,128]{0,2,1:T(8,128)(2,1)}, bf16[1312,8,128]{0,2,1:T(8,128)(2,1)S(1)}, u32[]{:S(2)}) copy-start(bf16[1312,8,128]{0,2,1:T(8,128)(2,1)S(1)} %get-tuple-element.610) | copy-start | bytes 8060932 | tf_op jit(solution)/shard_map/while
  905.1 14.0 copy-start.1
  1019.4 455.2 %reduce-scatter.13.cloned.1.call-start = ((), (), s32[]{:S(2)}) async-start(), calls=%async_computation.9 | async-start | bytes 1327104 | tf_op jit(solution)/shard_map/reduce_scatter | solution.py:276
  1024.7 465.6 %reduce-scatter.17.cloned.1.call-start = ((), (), s32[]{:S(2)}) async-start(), calls=%async_computation.11 | async-start | bytes 5308416 | tf_op jit(solution)/shard_map/reduce_scatter | solution.py:294
  1037.4 510.0 %reduce-scatter.15.cloned.1.call-start = ((), (), s32[]{:S(2)}) async-start(), calls=%async_computation.10 | async-start | bytes 5308416 | tf_op jit(solution)/shard_map/reduce_scatter | solution.py:288
  1053.1 546.2 %reduce-scatter.11.cloned.1.call-start = ((), (), s32[]{:S(2)}) async-start(), calls=%async_computation.8 | async-start | bytes 3981312 | tf_op jit(solution)/shard_map/reduce_scatter | solution.py:270
  1057.5 340.0 %copy-start.21 = (f32[1312]{0:T(1024)S(1)}, f32[1312]{0:T(1024)}, u32[]{:S(2)}) copy-start(f32[1312]{0:T(1024)} %copy-done.20) | copy-start | bytes 15748
  1406.4 230.3 %reduce-scatter.19.cloned.1.call-start = ((), (), s32[]{:S(2)}) async-start(), calls=%async_computation.12 | async-start | bytes 221184
  1440.0 276.1 %all-reduce.12.cloned.1.call-start = ((), (), s32[]{:S(2)}) async-start(), calls=%async_computation.13 | async-start | bytes 3538944 | tf_op jit(solution)/shard_map/psum | solution.py:308
  (81 other events, 434.5 us)
Sparse Core Ops, SparseCore 0:
  30.8 157.9 all-gather.1
  1019.5 372.0 reduce-scatter.8
  1395.4 36.7 reduce-scatter.12
  1435.9 54.3 reduce-scatter.16
  1493.6 53.8 reduce-scatter.14
  1551.2 48.0 reduce-scatter.10
  1603.2 33.4 reduce-scatter.18
  1639.4 76.6 all-reduce.11
where the time goes:
time: 1740 us; the launch traced here: 1730 us
  waiting for transfers between devices  687 us (39%)
  matrix products  398 us (23%)
  local copies, waits for them, and re-layouts  349 us (20%)
  other arithmetic  239 us (14%)
  blocking collectives  40.3 us (2%)
    reduce_scatter x1, waiting for transfers between devices, per_device(): lax.psum_scatter(grad_memory_all, ('freq', 'tm'), scatter_dimension=0, ti...  334 us
    all_gather x1, waiting for transfers between devices, per_device(): all_memory = lax.all_gather(key_value, ('freq', 'tm'), axis=0, tiled=True)  144 us
    dynamic_update_slice x12, other arithmetic, add_lanes(): return lax.dynamic_update_slice_in_dim(target, current + addend, offset, 2)  78.9 us
    dynamic_slice x36, local copies, waits for them, and re-layouts, head_pair(): section = lax.dynamic_slice_in_dim(array, offset, lane_width, 2)  78.8 us
    dot_general x4, matrix products, matmul(): return jnp.dot(left, right, preferred_element_type=jnp.float32)  68.8 us
    while x1, local copies, waits for them, and re-layouts, per_device(): lax.fori_loop(0, pair_count, backward_pair, (zero_query, jnp.zeros((key_c...  67.9 us
    dot_general x6, matrix products, pair_probs(): jnp.einsum('qchd,kchd->chqk', query_pair, key_pair, preferred_element_typ...  66.2 us
    convert_element_type x6, other arithmetic, query_side(): grad_scores = (probability * (grad_probs - delta)).astype(jnp.bfloat16)  62.9 us
  transfers between devices with their start and end apart: 8, of which 7 were waited for; matrix products, arithmetic and copies ran while one was open for 7% of the time, Pallas kernels for 0%

commit v1 on v0

--- a/solution.py
+++ b/solution.py
@@ -9,6 +9,19 @@
 FREQ_ROWS = 12
 EPS = 1e-06
 NEG = -1000000000.0
+
+
+def ring_gather(shard, axis, dim):
+    ways = lax.axis_size(axis)
+    up = [(d, (d + 1) % ways) for d in range(ways)]
+    down = [(d, (d - 1) % ways) for d in range(ways)]
+    earlier, later = ([shard], [shard])
+    for _ in range(ways // 2):
+        earlier.append(lax.ppermute(earlier[-1], axis, up))
+    for _ in range((ways - 1) // 2):
+        later.append(lax.ppermute(later[-1], axis, down))
+    line = jnp.concatenate([*earlier[::-1], *later[1:]], axis=dim)
+    return jnp.roll(line, (lax.axis_index(axis) - ways // 2) * shard.shape[dim], axis=dim)
 
 
 def live_slots(col_counts, slot_ids, freq_ids, time_ids, freq_rows, cap_cols):
@@ -130,7 +143,7 @@
     memory_low = (joint[:, 2 * width :] + bias_full[1]).astype(jnp.bfloat16)
     query3 = query_low.reshape(slots, clips, width)
     key_value = jnp.concatenate([keys_low, memory_low], axis=1).reshape(slots, clips, 2 * width)
-    all_memory = lax.all_gather(key_value, ("freq", "tm"), axis=0, tiled=True)
+    all_memory = ring_gather(key_value, ("freq", "tm"), 0)
 
     def forward_pair(number, state):
         mixed_acc, log_acc = state

time: 1740 us -> 2250 us (1.29)
  waiting for transfers between devices: 687 us -> 1100 us
  local copies, waits for them, and re-layouts: 349 us -> 429 us
    ppermute x0 -> x7, waiting for transfers between devices: none -> 560 us  [the longest x4 326 us: ring_gather(): earlier.append(lax.ppermute(earlier[-1], axis, up))]
    all_gather x1 -> x0, waiting for transfers between devices: 144 us -> none  [per_device(): all_memory = lax.all_gather(key_value, ('freq', 'tm'), axis=0, tiled=True)]
    unnamed x94 -> x127, local copies, waits for them, and re-layouts: 9.75 us -> 63 us
  transfers between devices with their start and end apart: 8 -> 14, of which waited for: 7 -> 13; matrix products, arithmetic and copies ran while one was open for 7% -> 6% of each run, Pallas kernels for 0% -> 0%
where the time goes in v1:
time: 2250 us; the launch traced here: 2240 us
  waiting for transfers between devices  1100 us (49%)
  local copies, waits for them, and re-layouts  429 us (19%)
  matrix products  397 us (18%)
  other arithmetic  242 us (11%)
  blocking collectives  40.4 us (2%)
    reduce_scatter x1, waiting for transfers between devices, per_device(): lax.psum_scatter(grad_memory_all, ('freq', 'tm'), scatter_dimension=0, ti...  335 us
    ppermute x4, waiting for transfers between devices, ring_gather(): earlier.append(lax.ppermute(earlier[-1], axis, up))  326 us
    ppermute x3, waiting for transfers between devices, ring_gather(): later.append(lax.ppermute(later[-1], axis, down))  234 us
    dynamic_update_slice x12, other arithmetic, add_lanes(): return lax.dynamic_update_slice_in_dim(target, current + addend, offset, 2)  78.9 us
    dynamic_slice x36, local copies, waits for them, and re-layouts, head_pair(): section = lax.dynamic_slice_in_dim(array, offset, lane_width, 2)  78.8 us
    dot_general x4, matrix products, matmul(): return jnp.dot(left, right, preferred_element_type=jnp.float32)  68.2 us
    while x1, local copies, waits for them, and re-layouts, per_device(): lax.fori_loop(0, pair_count, backward_pair, (zero_query, jnp.zeros((key_c...  67.7 us
    dot_general x6, matrix products, pair_probs(): jnp.einsum('qchd,kchd->chqk', query_pair, key_pair, preferred_element_typ...  66.2 us
  transfers between devices with their start and end apart: 14, of which 13 were waited for; matrix products, arithmetic and copies ran while one was open for 6% of the time, Pallas kernels for 0%

profile of v1, /device:TPU:0, one launch (start us, length us, event | category | flops | bytes accessed | tf_op | source)
XLA Modules:
  0.0 2240.2 jit_solution(2833543960884133687)
XLA Ops:
  33.3 87.2 %collective-permute-done = bf16[164,8,1536]{2,1,0:T(8,128)(2,1)S(1)} collective-permute-done((bf16[164,8,1536]{2,1,0:T(8,128)(2,1)S(1)}, bf16[164,8,1536]{2,1,0:T(8,128)(2,1)S(1)}, u32[]{:S(2)}, u32[]{:S(2)}) %collective-permute-start) | collective-permute-done | bytes 4030496 | tf_op jit(solution)/shard_map/ppermute | solution.py:20
  125.0 86.8 %collective-permute-done.1 = bf16[164,8,1536]{2,1,0:T(8,128)(2,1)S(1)} collective-permute-done((bf16[164,8,1536]{2,1,0:T(8,128)(2,1)S(1)}, bf16[164,8,1536]{2,1,0:T(8,128)(2,1)S(1)}, u32[]{:S(2)}, u32[]{:S(2)}) %collective-permute-start.1) | collective-permute-done | bytes 4030496 | tf_op jit(solution)/shard_map/ppermute | solution.py:20
  214.0 86.7 %collective-permute-done.4 = bf16[164,8,1536]{2,1,0:T(8,128)(2,1)S(1)} collective-permute-done((bf16[164,8,1536]{2,1,0:T(8,128)(2,1)S(1)}, bf16[164,8,1536]{2,1,0:T(8,128)(2,1)S(1)}, u32[]{:S(2)}, u32[]{:S(2)}) %collective-permute-start.4) | collective-permute-done | bytes 4030496 | tf_op jit(solution)/shard_map/ppermute | solution.py:22
  302.7 82.0 %collective-permute-done.2 = bf16[164,8,1536]{2,1,0:T(8,128)(2,1)} collective-permute-done((bf16[164,8,1536]{2,1,0:T(8,128)(2,1)S(1)}, bf16[164,8,1536]{2,1,0:T(8,128)(2,1)}, u32[]{:S(2)}, u32[]{:S(2)}) %collective-permute-start.2) | collective-permute-done | bytes 4030496 | tf_op jit(solution)/shard_map/ppermute | solution.py:20
  386.9 86.7 %collective-permute-done.5 = bf16[164,8,1536]{2,1,0:T(8,128)(2,1)} collective-permute-done((bf16[164,8,1536]{2,1,0:T(8,128)(2,1)S(1)}, bf16[164,8,1536]{2,1,0:T(8,128)(2,1)}, u32[]{:S(2)}, u32[]{:S(2)}) %collective-permute-start.5) | collective-permute-done | bytes 4030496 | tf_op jit(solution)/shard_map/ppermute | solution.py:22
  487.4 70.0 %collective-permute-done.3 = bf16[164,8,1536]{2,1,0:T(8,128)(2,1)} collective-permute-done((bf16[164,8,1536]{2,1,0:T(8,128)(2,1)}, bf16[164,8,1536]{2,1,0:T(8,128)(2,1)}, u32[]{:S(2)}, u32[]{:S(2)}) %collective-permute-start.3) | collective-permute-done | bytes 4030496 | tf_op jit(solution)/shard_map/ppermute | solution.py:20
  583.6 60.6 %collective-permute-done.6 = bf16[164,8,1536]{2,1,0:T(8,128)(2,1)} collective-permute-done((bf16[164,8,1536]{2,1,0:T(8,128)(2,1)}, bf16[164,8,1536]{2,1,0:T(8,128)(2,1)}, u32[]{:S(2)}, u32[]{:S(2)}) %collective-permute-start.6) | collective-permute-done | bytes 4030496 | tf_op jit(solution)/shard_map/ppermute | solution.py:22
  675.0 22.1 constant_dynamic-slice_fusion.8
  697.1 42.4 %copy.48 = bf16[1312,8,1536]{0,2,1:T(8,128)(2,1)} copy(bf16[1312,8,1536]{2,1,0:T(8,128)(2,1)} %constant_dynamic-slice_fusion.8) | data formatting | bytes 64487424 | tf_op jit(solution)/shard_map/while | solution.py:173
  740.2 122.8 %while.34 = (s32[]{:T(128)}, bf16[164,8,768]{2,1,0:T(8,128)(2,1)}, f32[164,8,12]{0,2,1:T(8,128)}, bf16[1312,8,1536]{0,2,1:T(8,128)(2,1)}, bf16[164,8,768]{0,2,1:...) while((s32[]{:T(128)}, bf16[164,8,768]{2,1,0:T(8,128)(2,1)}, ...), condition=%wide.region_6.7_spmd, body=%wide.region_3.6_spmd.sunk | while | flops 922637760 | bytes 60295916 | solution.py:173
  868.9 45.3 %multiply_convert_fusion.1 = (bf16[1312,3072]{1,0:T(8,128)(2,1)}, f32[1312,3072]{1,0:T(8,128)}, f32[1312,3072]{1,0:T(8,128)}) fusion(f32[3072]{0:T(1024)S(1)} %copy-done.51, bf16[768,3072]{1,0:T(8,128)(2,1)S(1)} %bitcast.208, f32[1312,768]{1,0:T(8,128)S(1)} %get-tuple-element.504, f32[768]{0:T(1024)S(1)} %copy-done.56, f32[768]{0:T(1024)S(1)} %copy-done.49, ...), kind=kOutput, calls=%fused_computation.34 | convolution fusion | flops 6461841408 | bytes 49082624 | tf_op jit(solution)/shard_map/dot_general | solution.py:49
  914.2 21.6 fusion.75
  935.8 14.1 multiply_reduce_fusion.1
  959.1 21.7 broadcast_in_dim.96
  980.8 478.8 %while.35 = (s32[]{:T(128)}, f32[164,8,768]{2,1,0:T(8,128)}, f32[1312,8,1536]{0,2,1:T(8,128)}, bf16[1312,8,1536]{0,2,1:T(8,128)(2,1)}, bf16[164,8,768]{0,2,1:T(8...) while((s32[]{:T(128)}, f32[164,8,768]{2,1,0:T(8,128)}, ...), condition=%wide.region_14.15_spmd, body=%wide.region_12.14_spmd.sunk | while | flops 2238668288 | bytes 267073456 | solution.py:259
  1003.6 11.0 multiply_reduce_fusion.5
  1163.0 11.0 multiply_reduce_fusion.5
  1242.8 11.0 multiply_reduce_fusion.5
  1322.5 11.0 multiply_reduce_fusion.5
  1402.2 11.0 multiply_reduce_fusion.5
  1459.5 67.7 %copy.55 = f32[1312,8,1536]{2,1,0:T(8,128)} copy(f32[1312,8,1536]{0,2,1:T(8,128)} %get-tuple-element.368) | data formatting | bytes 128974848 | tf_op jit(solution)/shard_map/while | solution.py:259
  1532.7 13.0 convolution_convert_fusion.2
  1546.3 15.1 convolution_convert_fusion.1
  1565.8 334.8 %reduce-scatter.9.cloned.1.call-done = f32[164,8,1536]{2,1,0:T(8,128)} async-done(((f32[1312,8,1536]{2,1,0:T(8,128)}), f32[164,8,1536]{2,1,0:T(8,128)}) %reduce-scatter.9.cloned.1.call-update) | async-done | bytes 8060944 | tf_op jit(solution)/shard_map/reduce_scatter | solution.py:265
  1923.4 11.5 fusion.40
  1954.9 27.6 %all-reduce.7 = (bf16[768]{0:T(1024)(128)(2,1)}, bf16[768]{0:T(1024)(128)(2,1)}, bf16[768]{0:T(1024)(128)(2,1)}, bf16[768]{0:T(1024)(128)(2,1)}, bf16[3072]{0:T(...) all-reduce(bf16[768]{0:T(1024)(128)(2,1)} %get-tuple-element.425, ...), channel_id=4, replica_groups=mesh['dp'=4,'freq'=2,'tm'=4] {'freq','tm'}, use_global_device_ids=true, to_apply=%region_22.23.clone | all-reduce | flops 7680 | bytes 30720
  1983.8 15.7 reduce-scatter.17.cloned.1.call-done
  1999.5 57.2 %reduce-scatter.15.cloned.1.call-done = bf16[96,3072]{1,0:T(8,128)(2,1)} async-done(((bf16[768,3072]{1,0:T(8,128)(2,1)}), bf16[96,3072]{1,0:T(8,128)(2,1)}) %reduce-scatter.15.cloned.1.call-update) | async-done | bytes 589840 | tf_op jit(solution)/shard_map/reduce_scatter | solution.py:301
  2056.7 51.9 %reduce-scatter.11.cloned.1.call-done = bf16[96,2304]{1,0:T(8,128)(2,1)} async-done(((bf16[768,2304]{1,0:T(8,128)(2,1)}), bf16[96,2304]{1,0:T(8,128)(2,1)}) %reduce-scatter.11.cloned.1.call-update) | async-done | bytes 442384 | tf_op jit(solution)/shard_map/reduce_scatter | solution.py:283
  2123.6 22.2 reduce-scatter.19.cloned.1.call-done
  2146.6 12.7 all-reduce.8
  2164.2 60.9 %all-reduce.12.cloned.1.call-done = (bf16[96,2304]{1,0:T(8,128)(2,1)}, bf16[96,768]{1,0:T(8,128)(2,1)}, bf16[96,3072]{1,0:T(8,128)(2,1)}, bf16[384,768]{1,0:T(8,128)(2,1)}) async-done(((bf16[96,2304]{1,0:T(8,128)(2,1)}, bf16[96,768]{1,0:T(8,128)(2,1)}, bf16[96,3072]{1,0:T(8,128)(2,1)}, bf16[384,768]{1,0:T(8,128)(2,1)}), (bf16[96,2304]{1,0:T(8,128)(2,1)}, bf16[96,768]{1,0:T(8,128)(2,1)}, ...) | async-done | bytes 1769488 | tf_op jit(solution)/shard_map/psum | solution.py:321
  (500 shorter events, 749.7 us)
Async XLA Ops:
  7.2 1893.5 %reduce-scatter.9.cloned.1.call-start = ((), (), s32[]{:S(2)}) async-start(), calls=%async_computation.6 | async-start | bytes 72548352 | tf_op jit(solution)/shard_map/reduce_scatter | solution.py:265
  10.9 15.3 copy-start.30
  29.1 445.8 %copy-start.53 = (bf16[3072]{0:T(1024)(128)(2,1)S(1)}, bf16[3072]{0:T(1024)(128)(2,1)}, u32[]{:S(2)}) copy-start(bf16[3072]{0:T(1024)(128)(2,1)} %param.24) | copy-start | bytes 18436
  30.3 90.1 %collective-permute-start = (bf16[164,8,1536]{2,1,0:T(8,128)(2,1)S(1)}, bf16[164,8,1536]{2,1,0:T(8,128)(2,1)S(1)}, u32[]{:S(2)}, u32[]{:S(2)}) collective-permute-start(bf16[164,8,1536]{2,1,0:T(8,128)(2,1)S(1)} %maximum_bitcast_fusion), channel_id=1, source_target_pairs={{0,1},{1,2},{2,3},{3,4},{4,5},{5,6},{6,7},{7,0},{8,9},{9,10},{10,1... | collective-permute-start | bytes 12091400 | tf_op jit(solution)/shard_map/ppermute | solution.py:20
  122.4 89.5 %collective-permute-start.1 = (bf16[164,8,1536]{2,1,0:T(8,128)(2,1)S(1)}, bf16[164,8,1536]{2,1,0:T(8,128)(2,1)S(1)}, u32[]{:S(2)}, u32[]{:S(2)}) collective-permute-start(bf16[164,8,1536]{2,1,0:T(8,128)(2,1)S(1)} %collective-permute-done), channel_id=1, source_target_pairs={{0,1},{1,2},{2,3},{3,4},{4,5},{5,6},{6,7},{7,0},{8,9},{9,10},{10,1... | collective-permute-start | bytes 12091400 | tf_op jit(solution)/shard_map/ppermute | solution.py:20
  124.0 176.7 %collective-permute-start.4 = (bf16[164,8,1536]{2,1,0:T(8,128)(2,1)S(1)}, bf16[164,8,1536]{2,1,0:T(8,128)(2,1)S(1)}, u32[]{:S(2)}, u32[]{:S(2)}) collective-permute-start(bf16[164,8,1536]{2,1,0:T(8,128)(2,1)S(1)} %maximum_bitcast_fusion), channel_id=1, source_target_pairs={{0,7},{1,0},{2,1},{3,2},{4,3},{5,4},{6,5},{7,6},{8,15},{9,8},{10,9... | collective-permute-start | bytes 12091400 | tf_op jit(solution)/shard_map/ppermute | solution.py:22
  211.8 261.8 %copy-start.17 = (bf16[164,8,1536]{2,1,0:T(8,128)(2,1)}, bf16[164,8,1536]{2,1,0:T(8,128)(2,1)S(1)}, u32[]{:S(2)}) copy-start(bf16[164,8,1536]{2,1,0:T(8,128)(2,1)S(1)} %collective-permute-done.1) | copy-start | bytes 12091396
  211.8 172.8 %collective-permute-start.2 = (bf16[164,8,1536]{2,1,0:T(8,128)(2,1)S(1)}, bf16[164,8,1536]{2,1,0:T(8,128)(2,1)}, u32[]{:S(2)}, u32[]{:S(2)}) collective-permute-start(bf16[164,8,1536]{2,1,0:T(8,128)(2,1)S(1)} %collective-permute-done.1), channel_id=1, source_target_pairs={{0,1},{1,2},{2,3},{3,4},{4,5},{5,6},{6,7},{7,0},{8,9},{9,10},{10,1... | collective-permute-start | bytes 12091400 | tf_op jit(solution)/shard_map/ppermute | solution.py:20
  302.7 170.9 %collective-permute-start.5 = (bf16[164,8,1536]{2,1,0:T(8,128)(2,1)S(1)}, bf16[164,8,1536]{2,1,0:T(8,128)(2,1)}, u32[]{:S(2)}, u32[]{:S(2)}) collective-permute-start(bf16[164,8,1536]{2,1,0:T(8,128)(2,1)S(1)} %collective-permute-done.4), channel_id=1, source_target_pairs={{0,7},{1,0},{2,1},{3,2},{4,3},{5,4},{6,5},{7,6},{8,15},{9,8},{10,9... | collective-permute-start | bytes 12091400 | tf_op jit(solution)/shard_map/ppermute | solution.py:22
  384.7 172.7 %collective-permute-start.3 = (bf16[164,8,1536]{2,1,0:T(8,128)(2,1)}, bf16[164,8,1536]{2,1,0:T(8,128)(2,1)}, u32[]{:S(2)}, u32[]{:S(2)}) collective-permute-start(bf16[164,8,1536]{2,1,0:T(8,128)(2,1)} %collective-permute-done.2), channel_id=1, source_target_pairs={{0,1},{1,2},{2,3},{3,4},{4,5},{5,6},{6,7},{7,0},{8,9},{9,10},{10,1... | collective-permute-start | bytes 12091400 | tf_op jit(solution)/shard_map/ppermute | solution.py:20
  473.6 170.7 %collective-permute-start.6 = (bf16[164,8,1536]{2,1,0:T(8,128)(2,1)}, bf16[164,8,1536]{2,1,0:T(8,128)(2,1)}, u32[]{:S(2)}, u32[]{:S(2)}) collective-permute-start(bf16[164,8,1536]{2,1,0:T(8,128)(2,1)} %collective-permute-done.5), channel_id=1, source_target_pairs={{0,7},{1,0},{2,1},{3,2},{4,3},{5,4},{6,5},{7,6},{8,15},{9,8},{10,9... | collective-permute-start | bytes 12091400 | tf_op jit(solution)/shard_map/ppermute | solution.py:22
  867.6 46.6 %copy-start.19 = (f32[1312,768]{1,0:T(8,128)}, f32[1312,768]{1,0:T(8,128)S(1)}, u32[]{:S(2)}) copy-start(f32[1312,768]{1,0:T(8,128)S(1)} %get-tuple-element.504) | copy-start | bytes 12091396
  867.7 82.3 %copy-start.41 = (f32[1312]{0:T(1024)}, f32[1312]{0:T(1024)S(1)}, u32[]{:S(2)}) copy-start(f32[1312]{0:T(1024)S(1)} %broadcast_multiply_fusion.1) | copy-start | bytes 15748
  868.3 45.9 %copy-start.45 = (f32[1312]{0:T(1024)}, f32[1312]{0:T(1024)S(1)}, u32[]{:S(2)}) copy-start(f32[1312]{0:T(1024)S(1)} %fusion.60) | copy-start | bytes 15748
  868.9 45.3 %copy-start.32 = (f32[1312]{0:T(1024)S(1)}, f32[1312]{0:T(1024)}, u32[]{:S(2)}) copy-start(f32[1312]{0:T(1024)} %convert_element_type.232) | copy-start | bytes 15748
  935.8 14.2 copy-start.20
  935.8 14.2 copy-start.46
  935.8 14.2 copy-start.50
  959.1 21.7 copy-start.25
  995.9 18.7 copy-start.2
  1075.7 18.7 copy-start.2
  1155.4 18.7 copy-start.2
  1235.1 18.7 copy-start.2
  1314.9 18.7 copy-start.2
  1394.5 18.7 copy-start.2
  1527.3 456.5 %reduce-scatter.13.cloned.1.call-start = ((), (), s32[]{:S(2)}) async-start(), calls=%async_computation.8 | async-start | bytes 1327104 | tf_op jit(solution)/shard_map/reduce_scatter | solution.py:289
  1532.6 466.9 %reduce-scatter.17.cloned.1.call-start = ((), (), s32[]{:S(2)}) async-start(), calls=%async_computation.10 | async-start | bytes 5308416 | tf_op jit(solution)/shard_map/reduce_scatter | solution.py:307
  1545.6 511.0 %reduce-scatter.15.cloned.1.call-start = ((), (), s32[]{:S(2)}) async-start(), calls=%async_computation.9 | async-start | bytes 5308416 | tf_op jit(solution)/shard_map/reduce_scatter | solution.py:301
  1561.4 547.1 %reduce-scatter.11.cloned.1.call-start = ((), (), s32[]{:S(2)}) async-start(), calls=%async_computation.7 | async-start | bytes 3981312 | tf_op jit(solution)/shard_map/reduce_scatter | solution.py:283
  1565.8 340.7 %copy-start.31 = (f32[1312]{0:T(1024)S(1)}, f32[1312]{0:T(1024)}, u32[]{:S(2)}) copy-start(f32[1312]{0:T(1024)} %copy-done.30) | copy-start | bytes 15748
  1915.5 230.3 %reduce-scatter.19.cloned.1.call-start = ((), (), s32[]{:S(2)}) async-start(), calls=%async_computation.11 | async-start | bytes 221184
  1949.0 276.1 %all-reduce.12.cloned.1.call-start = ((), (), s32[]{:S(2)}) async-start(), calls=%async_computation.12 | async-start | bytes 3538944 | tf_op jit(solution)/shard_map/psum | solution.py:321
  (97 other events, 563.9 us)
Sparse Core Ops, SparseCore 0:
  1527.4 373.2 reduce-scatter.8
  1904.5 36.7 reduce-scatter.12
  1945.1 54.3 reduce-scatter.16
  2002.8 53.8 reduce-scatter.14
  2060.4 48.0 reduce-scatter.10
  2112.3 33.4 reduce-scatter.18
  2148.5 76.5 all-reduce.11
